TPU v7x, 32 devices: a whole 2x2x4 slice. The times are simulated.
32 devices in a mesh: dp: 16 (over z, y, core), mp: 2 (over x).
Axes of the slice: x: 2, y: 2, z: 4, core: 2. Of those that a mesh axis runs over, the one named last changes fastest.
Arguments:
- tokens: bfloat16 [2048, 2048], P('dp', 'mp'), may hold values from -32 to 32
- lengths: int32 [4], replicated, may hold values from 1 to 1536, 2048 in all
- keep_mask: int32 [2048], replicated, may hold values 0 or 1
- routes: int32 [2048, 8], P('dp'), may hold values from 0 to 63, all different within a row; in each aligned block of 128 rows (0 to 127, 128 to 255, ...) at most 32 rows name the same one
- attention_gain: float32 [2048], replicated, may hold values from 0.1 to 1.9
- mixture_gain: float32 [2048], P('mp'), may hold values from 0.1 to 1.9
- query_gain: float32 [128], replicated, may hold values from 0.5 to 8, as said below
- key_gain: float32 [128], replicated, may hold values from 0.5 to 8, as said below
- query_weight: bfloat16 [2048, 2048], P('dp', 'mp'), may hold values from -0.125 to 0.125
- key_weight: bfloat16 [2048, 2048], P('dp', 'mp'), may hold values from -0.125 to 0.125
- value_weight: bfloat16 [2048, 2048], P('dp', 'mp'), may hold values from -0.125 to 0.125
- output_weight: bfloat16 [2048, 2048], P('mp', 'dp'), may hold values from -0.1875 to 0.1875
- router_weight: float32 [2048, 64], P('mp'), may hold values from -0.125 to 0.125
- expert_gate: bfloat16 [16, 2048, 4096], P('dp', None, 'mp'), may hold values from -0.125 to 0.125
- expert_up: bfloat16 [16, 2048, 4096], P('dp', None, 'mp'), may hold values from -0.125 to 0.125
- expert_down: bfloat16 [16, 4096, 2048], P('dp', 'mp'), may hold values from -0.25 to 0.25
Outputs:
- layer_output: bfloat16 [2048, 2048], P('dp', 'mp')
Inputs may be any that keep to these rules, and one draw needn't show every extreme that they name: The lengths sum to 2048; exactly one is 1536. `routes`: each row names 8 different experts. Within each aligned block of 128 rows (the rows of one index of dp) no expert is named by more than 32 rows, a bound that some block reaches. `query_gain`: Positive. `key_gain`: Positive.
All inputs are finite; a program needn't handle non-finite values.
Results may differ from a plain program's by a relative error of at most 0.012.
The roundings to bfloat16 on the way count: a program that leaves them out, or rounds other values in their place, can miss the bound.
Values may be sent and summed in bfloat16 or wider, within the bound.
A program may use at most 128 MiB of HBM per device.

v0:
```python
import jax
import jax.numpy as jnp
from jax import lax
from jax.sharding import PartitionSpec as P

D = 2048
HEAD_DIM = 128
FF = 1024
EXPERTS = 64
TOPK = 8
CAP = 32
EPS = 1e-06
ROPE_BASE = 10000.0
NEG = -1e30


def rope_tables(position):
    halves = HEAD_DIM // 2
    exponent = jnp.arange(halves, dtype=jnp.float32) * (2.0 / HEAD_DIM)
    frequency = jnp.power(jnp.float32(ROPE_BASE), -exponent)
    angle = position.astype(jnp.float32)[:, None] * frequency[None, :]
    cos_table = jnp.cos(angle)
    sin_table = jnp.sin(angle)
    return (jnp.concatenate([cos_table, cos_table], 1), jnp.concatenate([sin_table, sin_table], 1))


def head_prep(projected, head_gain, cos_table, sin_table):
    row_count = projected.shape[0]
    per_head = projected.reshape(row_count, -1, HEAD_DIM)
    normed = (
        per_head * lax.rsqrt(jnp.mean(per_head * per_head, axis=2, keepdims=True) + EPS) * head_gain
    )
    halves = HEAD_DIM // 2
    rotated = jnp.concatenate([-normed[:, :, halves:], normed[:, :, :halves]], 2)
    turned = normed * cos_table[:, None, :] + rotated * sin_table[:, None, :]
    return turned.reshape(row_count, -1).astype(jnp.bfloat16)


def segment_info(lengths, global_row):
    request_end = jnp.cumsum(lengths)
    request_start = request_end - lengths
    segment = jnp.sum((request_end[None, :] <= global_row[:, None]).astype(jnp.int32), axis=1)
    chosen = segment[:, None] == jnp.arange(lengths.shape[0], dtype=jnp.int32)[None, :]
    begin = jnp.sum(jnp.where(chosen, request_start[None, :], 0), axis=1)
    return (segment, global_row - begin)


def gather_tokens(block):
    return lax.all_gather(block, "dp", axis=0, tiled=True)


def attention(queries, keys, values, query_seg, query_row, key_seg, key_row, keep_mask):
    scale = HEAD_DIM ** (-0.5)
    scores = (
        lax.dot_general(queries, keys, (((1,), (1,)), ((), ())), preferred_element_type=jnp.float32)
        * scale
    )
    visible = (query_seg[:, None] == key_seg[None, :]) & (
        (keep_mask[None, :] == 1) | (query_row[:, None] == key_row[None, :])
    )
    masked = jnp.where(visible, scores, NEG)
    top = jnp.max(masked, axis=1, keepdims=True)
    weights = jnp.where(visible, jnp.exp(masked - top), 0.0)
    totals = jnp.sum(weights, axis=1, keepdims=True)
    mixed = jnp.dot(weights.astype(jnp.bfloat16), values, preferred_element_type=jnp.float32)
    return (mixed / totals).astype(jnp.bfloat16)


def local(
    tokens,
    lengths,
    keep_mask,
    routes,
    attention_gain,
    mixture_gain,
    query_gain,
    key_gain,
    query_weight,
    key_weight,
    value_weight,
    output_weight,
    router_weight,
    expert_gate,
    expert_up,
    expert_down,
):
    tok_rows = tokens.shape[0]
    dp_count = lax.axis_size("dp")
    dp_index = lax.axis_index("dp")
    mp_index = lax.axis_index("mp")
    local_width = query_weight.shape[1]
    local_heads = local_width // HEAD_DIM
    share = dp_count // local_heads
    part = dp_index % share
    total_rows = tok_rows * dp_count
    weight_rows = query_weight.shape[0]
    packed = jnp.stack([query_weight, key_weight, value_weight]).reshape(
        3, weight_rows, local_heads, HEAD_DIM
    )
    packed = packed.transpose(2, 1, 0, 3).reshape(local_heads, weight_rows, 3 * HEAD_DIM)
    packed = jnp.repeat(packed, share, axis=0)
    head_weight = lax.all_to_all(packed, "dp", split_axis=0, concat_axis=0, tiled=True)
    head_weight = head_weight.reshape(dp_count * weight_rows, 3 * HEAD_DIM)
    full_tokens = lax.all_gather(tokens, "mp", axis=1, tiled=True)
    xfloat = full_tokens.astype(jnp.float32)
    normed_in = (
        xfloat * lax.rsqrt(jnp.mean(xfloat * xfloat, axis=1, keepdims=True) + EPS) * attention_gain
    ).astype(jnp.bfloat16)
    all_in = gather_tokens(normed_in)
    all_output_weight = lax.all_gather(output_weight, "dp", axis=1, tiled=True)
    key_row = jnp.arange(total_rows, dtype=jnp.int32)
    key_seg, key_pos = segment_info(lengths, key_row)
    cos_table, sin_table = rope_tables(key_pos)

    def own(array):
        split = array.reshape((local_heads, share, tok_rows) + array.shape[1:])
        taken = lax.dynamic_index_in_dim(split, part, 1, keepdims=False)
        return taken.reshape((local_heads * tok_rows,) + array.shape[1:])

    projected = jnp.dot(all_in, head_weight, preferred_element_type=jnp.float32)
    queries = head_prep(own(projected[:, :HEAD_DIM]), query_gain, own(cos_table), own(sin_table))
    keys = head_prep(projected[:, HEAD_DIM : 2 * HEAD_DIM], key_gain, cos_table, sin_table)
    values = projected[:, 2 * HEAD_DIM :].astype(jnp.bfloat16)
    attended = attention(
        queries, keys, values, own(key_seg), own(key_row), key_seg, key_row, keep_mask
    )
    groups = [[head * share + p for head in range(local_heads)] for p in range(share)]
    attended = lax.all_to_all(
        attended.reshape(local_heads, tok_rows, HEAD_DIM),
        "dp",
        split_axis=0,
        concat_axis=0,
        tiled=True,
        axis_index_groups=groups,
    )
    attended = attended.transpose(1, 0, 2).reshape(tok_rows, local_width)
    partial_out = jnp.dot(attended, all_output_weight, preferred_element_type=jnp.float32)
    summed_out = lax.psum_scatter(partial_out, "mp", scatter_dimension=1, tiled=True)
    residual = (tokens.astype(jnp.float32) + summed_out).astype(jnp.bfloat16)
    hfloat = residual.astype(jnp.float32)
    scaled = hfloat * mixture_gain
    partial_logits = jnp.dot(scaled, router_weight, precision=lax.Precision.HIGHEST)
    square_sum, logit_sum = lax.psum((jnp.sum(hfloat * hfloat, axis=1), partial_logits), "mp")
    inverse = lax.rsqrt(square_sum / D + EPS)[:, None]
    mixed_in = (scaled * inverse).astype(jnp.bfloat16)
    logits = logit_sum * inverse
    experts = jnp.arange(EXPERTS, dtype=jnp.int32)
    named = jnp.any(routes[None, :, :] == experts[:, None, None], axis=2)
    named_float = named.astype(jnp.float32)
    sigmoid_vals = jax.nn.sigmoid(logits).T * named_float
    route_weight = sigmoid_vals / jnp.sum(sigmoid_vals, axis=0, keepdims=True)
    ids = jnp.arange(tok_rows, dtype=jnp.int32)
    earlier = (ids[:, None] < ids[None, :]).astype(jnp.bfloat16)
    before = jnp.dot(named.astype(jnp.bfloat16), earlier, preferred_element_type=jnp.float32)
    place = jnp.where(named, before.astype(jnp.int32), -1)
    exp_local = EXPERTS // dp_count
    gate_local = expert_gate[0]
    up_local = expert_up[0]
    down_local = expert_down[0]
    unit_count = gate_local.shape[1]
    held = max(1, unit_count // FF)
    units = unit_count // held
    first_expert = mp_index * unit_count // FF

    def mine(table):
        split = table.reshape(dp_count, exp_local, tok_rows)
        return lax.dynamic_slice_in_dim(split, first_expert, held, 1)

    slots = jnp.arange(CAP, dtype=jnp.int32)
    chosen = mine(place)[:, :, None, :] == slots[None, None, :, None]
    select = chosen.astype(jnp.bfloat16).reshape(dp_count * held * CAP, tok_rows)
    full_in = lax.all_gather(mixed_in, "mp", axis=1, tiled=True)
    sending = jnp.dot(select, full_in, preferred_element_type=jnp.float32).astype(jnp.bfloat16)
    rows_in = lax.all_to_all(
        sending.reshape(dp_count, held, CAP, D), "dp", split_axis=0, concat_axis=0, tiled=True
    )
    outs = []
    for index in range(held):
        rows = rows_in[:, index].reshape(dp_count * CAP, D)
        low, high = (index * units, (index + 1) * units)
        gate_val = jnp.dot(rows, gate_local[:, low:high], preferred_element_type=jnp.float32)
        up_val = jnp.dot(rows, up_local[:, low:high], preferred_element_type=jnp.float32)
        hidden = (jax.nn.silu(gate_val) * up_val).astype(jnp.bfloat16)
        out = jnp.dot(hidden, down_local[low:high], preferred_element_type=jnp.float32)
        outs.append(out.astype(jnp.bfloat16).reshape(dp_count, CAP, D))
    returned = lax.all_to_all(
        jnp.stack(outs, axis=1), "dp", split_axis=0, concat_axis=0, tiled=True
    ).reshape(dp_count * held * CAP, D)
    spread = jnp.where(chosen, mine(route_weight)[:, :, None, :], 0.0)
    spread = spread.reshape(dp_count * held * CAP, tok_rows)
    spread_high = spread.astype(jnp.bfloat16)
    spread_mid = (spread - spread_high.astype(jnp.float32)).astype(jnp.bfloat16)
    contract = (((0,), (0,)), ((), ()))
    mixture = lax.dot_general(
        spread_high, returned, contract, preferred_element_type=jnp.float32
    ) + lax.dot_general(spread_mid, returned, contract, preferred_element_type=jnp.float32)
    mixture = lax.psum_scatter(mixture, "mp", scatter_dimension=1, tiled=True)
    return (hfloat + mixture).astype(jnp.bfloat16)


def solution(mesh):
    return jax.shard_map(
        local,
        mesh=mesh,
        in_specs=(
            P("dp", "mp"),
            P(),
            P(),
            P("dp", None),
            P(),
            P("mp"),
            P(),
            P(),
            P("dp", "mp"),
            P("dp", "mp"),
            P("dp", "mp"),
            P("mp", "dp"),
            P("mp", None),
            P("dp", None, "mp"),
            P("dp", None, "mp"),
            P("dp", "mp", None),
        ),
        out_specs=P("dp", "mp"),
        check_vma=False,
    )
```

profile of v0, /device:TPU:0, one launch (start us, length us, event | category | flops | bytes accessed | tf_op | source)
XLA Modules:
  0.0 488.3 jit_solution(367880626133548728)
XLA Ops:
  6.5 10.3 %all_gather.12 = bf16[128,2048]{1,0:T(8,128)(2,1)S(1)} all-gather(bf16[128,1024]{1,0:T(8,128)(2,1)} %param.16), channel_id=1, replica_groups=mesh['dp'=16,'mp'=2] {'mp'}, dimensions={1}, use_global_device_ids=true | all-gather | bytes 786432 | tf_op jit(solution)/shard_map/all_gather | solution.py:104
  17.0 1.7 fusion.35
  24.0 6.2 %all-to-all-start = ((bf16[16,128,384]{2,1,0:T(8,128)(2,1)}), bf16[16,128,384]{2,1,0:T(8,128)(2,1)}, u32[]{:S(2)}, u32[]{:S(2)}) async-start(bf16[16,128,384]{2,1,0:T(8,128)(2,1)} %bitcast.10), calls=%async_computation | async-start | bytes 3145728 | tf_op jit(solution)/shard_map/all_to_all | solution.py:102
  31.5 3.7 multiply_cosine_fusion
  35.2 3.3 multiply_sine_fusion.1
  38.4 39.1 %all-to-all-done = bf16[16,128,384]{2,1,0:T(8,128)(2,1)} async-done(((bf16[16,128,384]{2,1,0:T(8,128)(2,1)}), bf16[16,128,384]{2,1,0:T(8,128)(2,1)}, u32[]{:S(2)}, u32[]{:S(2)}) %all-to-all-start) | async-done | bytes 1572896 | tf_op jit(solution)/shard_map/all_to_all | solution.py:102
  77.6 43.2 %all-gather.3.cloned.1.call-done = bf16[2048,2048]{1,0:T(8,128)(2,1)} async-done(((bf16[128,2048]{1,0:T(8,128)(2,1)}), bf16[2048,2048]{1,0:T(8,128)(2,1)}) %all-gather.3.cloned.1.call-update) | async-done | bytes 8388624 | tf_op jit(solution)/shard_map/all_gather | solution.py:49
  120.7 6.4 %fusion.88 = f32[2048,384]{0,1:T(8,128)S(1)} fusion(bf16[2048,2048]{1,0:T(8,128)(2,1)} %all-gather.3.cloned.1.call-done, bf16[2048,384]{1,0:T(8,128)(2,1)} %bitcast.11), kind=kOutput, calls=%fused_computation.130 | convolution fusion | flops 3221225472 | bytes 13107200 | tf_op jit(solution)/shard_map/dot_general | solution.py:120
  130.0 1.9 reshape.358
  131.9 1.7 constant_dynamic-slice_fusion.2
  136.6 3.4 fusion.2
  140.1 5.0 %fusion.3 = f32[1024]{0:T(1024)S(1)} fusion(f32[1024,2048]{1,0:T(8,128)S(1)} %get-tuple-element.24, f32[1024]{0:T(1024)S(1)} %get-tuple-element.23, s32[1024]{0:T(1024)S(1)} %bitcast.112, pred[2048]{0:T(1024)(128)(4,1)S(1)} %broadcast_compare_fusion, s32[2048]{0:T(1024)S(1)} %convert_reduce_fusion, s32[1024]{0:T(1024)S(1)} %bitcast.115), kind=kLoop, calls=%fused_computation.6 | loop fusion | flops 18873344 | bytes 8415232 | tf_op jit(solution)/shard_map/reduce_sum | solution.py:64
  145.0 3.9 fusion.45
  149.8 3.5 all-to-all-start.1
  153.4 24.8 %all-gather.5.cloned.1.call-done = bf16[1024,2048]{1,0:T(8,128)(2,1)} async-done(((bf16[1024,128]{1,0:T(8,128)(2,1)}), bf16[1024,2048]{1,0:T(8,128)(2,1)}) %all-gather.5.cloned.1.call-update) | async-done | bytes 4194320 | tf_op jit(solution)/shard_map/all_gather | solution.py:110
  178.2 3.9 fusion.89
  182.7 20.2 %reduce-scatter.3.cloned.1.call-done = f32[128,1024]{1,0:T(8,128)} async-done(((f32[128,2048]{1,0:T(8,128)}), f32[128,1024]{1,0:T(8,128)}) %reduce-scatter.3.cloned.1.call-update) | async-done | bytes 524304 | tf_op jit(solution)/shard_map/reduce_scatter | solution.py:138
  204.8 7.3 %all-reduce = (f32[128]{0:T(128)S(1)}, f32[128,64]{0,1:T(8,128)S(1)}) all-reduce(f32[128]{0:T(128)S(1)} %get-tuple-element.7, f32[128,64]{0,1:T(8,128)S(1)} %fusion.50), channel_id=1, replica_groups=mesh['dp'=16,'mp'=2] {'mp'}, use_global_device_ids=true, to_apply=%region_12.13 | all-reduce | flops 8320 | bytes 66560 | tf_op jit(solution)/shard_map/psum | solution.py:143
  212.2 7.0 %all_gather.15 = bf16[128,2048]{1,0:T(8,128)(2,1)S(1)} all-gather(bf16[128,1024]{1,0:T(8,128)(2,1)S(1)} %fusion.51), channel_id=1, replica_groups=mesh['dp'=16,'mp'=2] {'mp'}, dimensions={1}, use_global_device_ids=true | all-gather | bytes 786432 | tf_op jit(solution)/shard_map/all_gather | solution.py:172
  220.5 98.4 %all_to_all.20 = bf16[16,2,32,2048]{3,2,1,0:T(8,128)(2,1)S(1)} all-to-all(bf16[16,2,32,2048]{3,2,1,0:T(8,128)(2,1)S(1)} %bitcast.92), channel_id=1, replica_groups=mesh['dp'=16,'mp'=2] {'dp'}, dimensions={0} | all-to-all | bytes 8388608 | tf_op jit(solution)/shard_map/all_to_all | solution.py:174
  319.4 2.5 slice-done.1
  321.9 3.7 fusion.11
  325.6 3.7 fusion.7
  329.3 10.5 %fusion.21 = bf16[512,2048]{1,0:T(8,128)(2,1)} fusion(bf16[1,2048,2048]{2,1,0:T(8,128)(2,1)} %param.31, f32[512,1024]{1,0:T(8,128)} %fusion.11, bf16[512,2048]{1,0:T(8,128)(2,1)} %bitcast.99, bf16[2048,2048]{1,0:T(8,128)(2,1)} %bitcast.123), kind=kOutput, calls=%fused_computation.25 | convolution fusion | flops 4299161600 | bytes 14680064 | tf_op jit(solution)/shard_map/dot_general | solution.py:184
  339.9 9.9 %fusion.24 = bf16[512,2048]{1,0:T(8,128)(2,1)} fusion(bf16[1,2048,2048]{2,1,0:T(8,128)(2,1)} %param.31, f32[512,1024]{1,0:T(8,128)} %fusion.7, bf16[512,2048]{1,0:T(8,128)(2,1)S(1)} %bitcast.97, bf16[2048,2048]{1,0:T(8,128)(2,1)} %bitcast.124), kind=kOutput, calls=%fused_computation.26 | convolution fusion | flops 4299161600 | bytes 14680064 | tf_op jit(solution)/shard_map/dot_general | solution.py:184
  349.8 4.6 pad_maximum_fusion
  354.4 5.3 %all-to-all-start.3 = ((bf16[16,2,32,2048]{3,2,1,0:T(8,128)(2,1)}), bf16[16,2,32,2048]{3,2,1,0:T(8,128)(2,1)}, u32[]{:S(2)}, u32[]{:S(2)}) async-start(bf16[16,2,32,2048]{3,2,1,0:T(8,128)(2,1)} %pad_maximum_fusion), calls=%async_computation.4 | async-start | bytes 8388608 | tf_op jit(solution)/shard_map/all_to_all | solution.py:186
  359.9 77.5 %all-to-all-done.3 = bf16[16,2,32,2048]{3,2,1,0:T(8,128)(2,1)} async-done(((bf16[16,2,32,2048]{3,2,1,0:T(8,128)(2,1)}), bf16[16,2,32,2048]{3,2,1,0:T(8,128)(2,1)}, u32[]{:S(2)}, u32[]{:S(2)}) %all-to-all-start.3) | async-done | bytes 4194336 | tf_op jit(solution)/shard_map/all_to_all | solution.py:186
  437.4 3.0 convolution_bitcast_fusion
  440.4 3.9 fusion.27
  444.3 35.4 %reduce-scatter.5.cloned.1.call-done = f32[128,1024]{1,0:T(8,128)} async-done(((f32[128,2048]{1,0:T(8,128)}), f32[128,1024]{1,0:T(8,128)}) %reduce-scatter.5.cloned.1.call-update) | async-done | bytes 524304 | tf_op jit(solution)/shard_map/reduce_scatter | solution.py:197
  479.7 1.8 fusion.54
  (88 shorter events, 17.7 us)
Async XLA Ops:
  6.5 197.6 %copy-start = (f32[1024,64]{0,1:T(8,128)S(1)}, f32[1024,64]{0,1:T(8,128)}, u32[]{:S(2)}) copy-start(f32[1024,64]{0,1:T(8,128)} %param.28) | copy-start | bytes 786436
  6.5 114.2 %all-gather.3.cloned.1.call-start = ((), (), s32[]{:S(2)}) async-start(), calls=%async_computation.6 | async-start | bytes 8912896 | tf_op jit(solution)/shard_map/all_gather | solution.py:49
  22.1 8.8 %copy-start.14 = (s32[4]{0:T(128)S(1)}, s32[4]{0:T(128)}, u32[]{:S(2)}) copy-start(s32[4]{0:T(128)} %param.17) | copy-start | bytes 52
  22.1 9.3 %copy-start.10 = (s32[2048]{0:T(1024)S(1)}, s32[2048]{0:T(1024)}, u32[]{:S(2)}) copy-start(s32[2048]{0:T(1024)} %param.18) | copy-start | bytes 24580
  24.0 53.6 %all-to-all-start = ((bf16[16,128,384]{2,1,0:T(8,128)(2,1)}), bf16[16,128,384]{2,1,0:T(8,128)(2,1)}, u32[]{:S(2)}, u32[]{:S(2)}) async-start(bf16[16,128,384]{2,1,0:T(8,128)(2,1)} %bitcast.10), calls=%async_computation | async-start | bytes 3145728 | tf_op jit(solution)/shard_map/all_to_all | solution.py:102
  30.2 148.0 %all-gather.5.cloned.1.call-start = ((), (), s32[]{:S(2)}) async-start(), calls=%async_computation.7 | async-start | bytes 4456448 | tf_op jit(solution)/shard_map/all_gather | solution.py:110
  120.7 8.0 %copy-start.13 = (f32[128]{0:T(128)S(1)}, f32[128]{0:T(128)}, u32[]{:S(2)}) copy-start(f32[128]{0:T(128)} %param.23) | copy-start | bytes 1540
  127.1 1.7 copy-start.3
  128.8 5.4 %copy-start.12 = (f32[128]{0:T(128)S(1)}, f32[128]{0:T(128)}, u32[]{:S(2)}) copy-start(f32[128]{0:T(128)} %param.22) | copy-start | bytes 1540
  134.0 1.3 copy-start.2
  134.4 2.0 copy-start.4
  134.4 2.1 copy-start.7
  134.4 2.2 copy-start.8
  148.9 33.4 %copy-start.11 = (s32[128,8]{0,1:T(8,128)S(1)}, s32[128,8]{0,1:T(8,128)}, u32[]{:S(2)}) copy-start(s32[128,8]{0,1:T(8,128)} %param.19) | copy-start | bytes 12292
  148.9 54.0 %copy-start.6 = (bf16[128,1024]{1,0:T(8,128)(2,1)S(1)}, bf16[128,1024]{1,0:T(8,128)(2,1)}, u32[]{:S(2)}) copy-start(bf16[128,1024]{1,0:T(8,128)(2,1)} %param.16) | copy-start | bytes 786436
  149.8 54.4 %copy-start.9 = (f32[1024]{0:T(1024)S(1)}, f32[1024]{0:T(1024)}, u32[]{:S(2)}) copy-start(f32[1024]{0:T(1024)} %param.21) | copy-start | bytes 12292
  149.8 28.4 %all-to-all-start.1 = ((bf16[8,128,128]{1,2,0:T(8,128)(2,1)}), bf16[8,128,128]{1,2,0:T(8,128)(2,1)S(1)}, u32[]{:S(2)}, u32[]{:S(2)}) async-start(bf16[8,128,128]{1,2,0:T(8,128)(2,1)} %copy.45), calls=%async_computation.1 | async-start | bytes 524288 | tf_op jit(solution)/shard_map/all_to_all | solution.py:128
  153.3 49.6 %reduce-scatter.3.cloned.1.call-start = ((), (), s32[]{:S(2)}) async-start(), calls=%async_computation.8 | async-start | bytes 1572864 | tf_op jit(solution)/shard_map/reduce_scatter | solution.py:138
  220.5 98.9 %slice-start = ((s8[8388608]{0:T(1024)(128)(4,1)}), s8[4194304]{0:T(1024)(128)(4,1)S(1)}, s32[]{:S(2)}) async-start(s8[8388608]{0:T(1024)(128)(4,1)} %bitcast.119), calls=%async_computation.10 | async-start | bytes 8388608
  318.9 2.9 slice-start.1
  319.4 6.2 %copy-start.5 = (bf16[16,1,32,2048]{3,2,1,0:T(8,128)(2,1)}, bf16[16,1,32,2048]{3,2,1,0:T(8,128)(2,1)S(1)}, u32[]{:S(2)}) copy-start(bf16[16,1,32,2048]{3,2,1,0:T(8,128)(2,1)S(1)} %get-tuple-element.9) | copy-start | bytes 6291460
  354.4 83.0 %all-to-all-start.3 = ((bf16[16,2,32,2048]{3,2,1,0:T(8,128)(2,1)}), bf16[16,2,32,2048]{3,2,1,0:T(8,128)(2,1)}, u32[]{:S(2)}, u32[]{:S(2)}) async-start(bf16[16,2,32,2048]{3,2,1,0:T(8,128)(2,1)} %pad_maximum_fusion), calls=%async_computation.4 | async-start | bytes 8388608 | tf_op jit(solution)/shard_map/all_to_all | solution.py:186
  359.7 120.0 %reduce-scatter.5.cloned.1.call-start = ((), (), s32[]{:S(2)}) async-start(), calls=%async_computation.9 | async-start | bytes 1572864 | tf_op jit(solution)/shard_map/reduce_scatter | solution.py:197
  437.4 44.1 %copy-start.1 = (f32[1024,64]{0,1:T(8,128)S(1)}, f32[1024,64]{0,1:T(8,128)}, u32[]{:S(2)}) copy-start(f32[1024,64]{0,1:T(8,128)} %param.28) | copy-start | bytes 786436
Sparse Core Ops, SparseCore 0:
  18.9 101.8 all-gather.2
  122.9 55.2 all-gather.4
  182.3 20.6 reduce-scatter.2
  444.4 35.2 reduce-scatter.4
where the time goes:
time: 494 us; the launch traced here: 488 us
  waiting for transfers between devices  241 us (49%)
  blocking collectives  123 us (25%)
  matrix products  54.4 us (11%)
  other arithmetic  25 us (5%)
  local copies, waits for them, and re-layouts  15.8 us (3%)
  starting transfers between devices  15.2 us (3%)
  between operations  13.8 us (3%)
    all_to_all x1, blocking collectives, local(): lax.all_to_all(sending.reshape(dp_count, held, CAP, D), 'dp', split_axis=...  98.4 us
    all_to_all x1, waiting for transfers between devices, local(): lax.all_to_all(jnp.stack(outs, axis=1), 'dp', split_axis=0, concat_axis=0...  77.5 us
    all_gather x1, waiting for transfers between devices, gather_tokens(): return lax.all_gather(block, 'dp', axis=0, tiled=True)  43.2 us
    all_to_all x1, waiting for transfers between devices, local(): lax.all_to_all(packed, 'dp', split_axis=0, concat_axis=0, tiled=True)  39.1 us
    reduce_scatter x1, waiting for transfers between devices, local(): mixture = lax.psum_scatter(mixture, 'mp', scatter_dimension=1, tiled=True)  35.4 us
    all_gather x1, waiting for transfers between devices, local(): all_output_weight = lax.all_gather(output_weight, 'dp', axis=1, tiled=True)  24.8 us
    dot_general x2, matrix products, local(): jnp.dot(hidden, down_local[low:high], preferred_element_type=jnp.float32)  20.5 us
    reduce_scatter x1, waiting for transfers between devices, local(): lax.psum_scatter(partial_out, 'mp', scatter_dimension=1, tiled=True)  20.2 us
  transfers between devices with their start and end apart: 7, of which 6 were waited for; matrix products, arithmetic and copies ran while one was open for 8% of the time, Pallas kernels for 0%

commit v1 on v0

--- a/solution.py
+++ b/solution.py
@@ -14,6 +14,22 @@
 NEG = -1e30
 
 
+def collect(x, axis, dim):
+    ways, here, step = (lax.axis_size(axis), lax.axis_index(axis), x.shape[dim])
+    lengths = [n * ways if d == dim else n for d, n in enumerate(x.shape)]
+    full = lax.dynamic_update_slice_in_dim(jnp.zeros(lengths, x.dtype), x, here * step, axis=dim)
+    going_up = going_down = x
+    for far in range(1, ways // 2 + 1):
+        going_up = lax.ppermute(going_up, axis, [(d, (d + 1) % ways) for d in range(ways)])
+        full = lax.dynamic_update_slice_in_dim(full, going_up, (here - far) % ways * step, axis=dim)
+        if 2 * far < ways:
+            going_down = lax.ppermute(going_down, axis, [(d, (d - 1) % ways) for d in range(ways)])
+            full = lax.dynamic_update_slice_in_dim(
+                full, going_down, (here + far) % ways * step, axis=dim
+            )
+    return full
+
+
 def rope_tables(position):
     halves = HEAD_DIM // 2
     exponent = jnp.arange(halves, dtype=jnp.float32) * (2.0 / HEAD_DIM)
@@ -46,7 +62,7 @@
 
 
 def gather_tokens(block):
-    return lax.all_gather(block, "dp", axis=0, tiled=True)
+    return collect(block, "dp", 0)
 
 
 def attention(queries, keys, values, query_seg, query_row, key_seg, key_row, keep_mask):

time: 494 us -> 527 us (1.067)
  waiting for transfers between devices: 241 us -> 205 us
  starting transfers between devices: 15.2 us -> 43.6 us
  local copies, waits for them, and re-layouts: 15.8 us -> 36.1 us
  blocking collectives: 123 us -> 142 us
    ppermute x0 -> x15, waiting for transfers between devices: none -> 73.2 us  [the longest x8 68.8 us: collect(): lax.ppermute(going_up, axis, [(d, (d + 1) % ways) for d in range(ways)])]
    all_gather x1 -> x0, waiting for transfers between devices: 43.2 us -> none  [gather_tokens(): return lax.all_gather(block, 'dp', axis=0, tiled=True)]
    all_to_all x1, waiting for transfers between devices: 39.1 us -> 0.01 us  [local(): lax.all_to_all(packed, 'dp', split_axis=0, concat_axis=0, tiled=True)]
    ppermute x0 -> x15, starting transfers between devices: none -> 33.7 us  [the longest x7 31.4 us: collect(): lax.ppermute(going_down, axis, [(d, (d - 1) % ways) for d in range(ways)])]
    all_gather x1, waiting for transfers between devices: 24.8 us -> 0.01 us  [local(): all_output_weight = lax.all_gather(output_weight, 'dp', axis=1, tiled=True)]
    all_to_all x0 -> x1, blocking collectives: none -> 19 us  [local(): lax.all_to_all(attended.reshape(local_heads, tok_rows, HEAD_DIM), 'dp', s...]
    dynamic_update_slice x0 -> x15, local copies, waits for them, and re-layouts: none -> 17.8 us  [the longest x8 9.88 us: collect(): lax.dynamic_update_slice_in_dim(full, going_up, (here - far) % ways * ste...]
  transfers between devices with their start and end apart: 7 -> 20, of which waited for: 6 -> 13; matrix products, arithmetic and copies ran while one was open for 8% -> 10% of each run, Pallas kernels for 0% -> 0%
where the time goes in v1:
time: 527 us; the launch traced here: 520 us
  waiting for transfers between devices  205 us (39%)
  blocking collectives  142 us (27%)
  matrix products  55.1 us (10%)
  starting transfers between devices  43.6 us (8%)
  local copies, waits for them, and re-layouts  36.1 us (7%)
  other arithmetic  23.8 us (5%)
  between operations  14.1 us (3%)
    all_to_all x1, blocking collectives, local(): lax.all_to_all(sending.reshape(dp_count, held, CAP, D), 'dp', split_axis=...  98.4 us
    all_to_all x1, waiting for transfers between devices, local(): lax.all_to_all(jnp.stack(outs, axis=1), 'dp', split_axis=0, concat_axis=0...  77.5 us
    ppermute x8, waiting for transfers between devices, collect(): lax.ppermute(going_up, axis, [(d, (d + 1) % ways) for d in range(ways)])  68.8 us
    reduce_scatter x1, waiting for transfers between devices, local(): mixture = lax.psum_scatter(mixture, 'mp', scatter_dimension=1, tiled=True)  35.4 us
    ppermute x7, starting transfers between devices, collect(): lax.ppermute(going_down, axis, [(d, (d - 1) % ways) for d in range(ways)])  31.4 us
    dot_general x2, matrix products, local(): jnp.dot(hidden, down_local[low:high], preferred_element_type=jnp.float32)  21.2 us
    all_to_all x1, blocking collectives, local(): lax.all_to_all(attended.reshape(local_heads, tok_rows, HEAD_DIM), 'dp', s...  19 us
    reduce_scatter x1, waiting for transfers between devices, local(): lax.psum_scatter(partial_out, 'mp', scatter_dimension=1, tiled=True)  18 us
  transfers between devices with their start and end apart: 20, of which 13 were waited for; matrix products, arithmetic and copies ran while one was open for 10% of the time, Pallas kernels for 0%

profile of v1, /device:TPU:0, one launch (start us, length us, event | category | flops | bytes accessed | tf_op | source)
XLA Modules:
  0.0 519.6 jit_solution(18368729937342853214)
XLA Ops:
  6.5 10.3 %all_gather.9 = bf16[128,2048]{1,0:T(8,128)(2,1)S(1)} all-gather(bf16[128,1024]{1,0:T(8,128)(2,1)} %param.16), channel_id=1, replica_groups=mesh['dp'=16,'mp'=2] {'mp'}, dimensions={1}, use_global_device_ids=true | all-gather | bytes 786432 | tf_op jit(solution)/shard_map/all_gather | solution.py:120
  17.1 4.3 broadcast_in_dim.34
  22.4 4.4 collective-permute-start.1
  30.1 4.4 all-to-all-start
  36.1 4.3 collective-permute-start.3
  43.1 36.9 %collective-permute-done.2 = bf16[128,2048]{1,0:T(8,128)(2,1)} collective-permute-done((bf16[128,2048]{1,0:T(8,128)(2,1)S(1)}, bf16[128,2048]{1,0:T(8,128)(2,1)}, u32[]{:S(2)}, u32[]{:S(2)}) %collective-permute-start.2) | collective-permute-done | bytes 524320 | tf_op jit(solution)/shard_map/ppermute | solution.py:23
  83.8 4.5 collective-permute-start.5
  88.3 6.7 %collective-permute-done.4 = bf16[128,2048]{1,0:T(8,128)(2,1)} collective-permute-done((bf16[128,2048]{1,0:T(8,128)(2,1)}, bf16[128,2048]{1,0:T(8,128)(2,1)}, u32[]{:S(2)}, u32[]{:S(2)}) %collective-permute-start.4) | collective-permute-done | bytes 524320 | tf_op jit(solution)/shard_map/ppermute | solution.py:23
  98.8 4.6 collective-permute-start.7
  104.3 5.9 %collective-permute-done.6 = bf16[128,2048]{1,0:T(8,128)(2,1)} collective-permute-done((bf16[128,2048]{1,0:T(8,128)(2,1)}, bf16[128,2048]{1,0:T(8,128)(2,1)}, u32[]{:S(2)}, u32[]{:S(2)}) %collective-permute-start.6) | collective-permute-done | bytes 524320 | tf_op jit(solution)/shard_map/ppermute | solution.py:23
  114.0 4.4 collective-permute-start.9
  120.3 7.1 %collective-permute-done.8 = bf16[128,2048]{1,0:T(8,128)(2,1)S(1)} collective-permute-done((bf16[128,2048]{1,0:T(8,128)(2,1)}, bf16[128,2048]{1,0:T(8,128)(2,1)S(1)}, u32[]{:S(2)}, u32[]{:S(2)}) %collective-permute-start.8) | collective-permute-done | bytes 524320 | tf_op jit(solution)/shard_map/ppermute | solution.py:23
  131.3 4.4 collective-permute-start.11
  142.4 4.7 collective-permute-start.13
  154.6 7.4 %collective-permute-done.14 = bf16[128,2048]{1,0:T(8,128)(2,1)S(1)} collective-permute-done((bf16[128,2048]{1,0:T(8,128)(2,1)S(1)}, bf16[128,2048]{1,0:T(8,128)(2,1)S(1)}, u32[]{:S(2)}, u32[]{:S(2)}) %collective-permute-start.14) | collective-permute-done | bytes 524320 | tf_op jit(solution)/shard_map/ppermute | solution.py:23
  162.9 6.4 %fusion.89 = f32[2048,384]{0,1:T(8,128)S(1)} fusion(bf16[2048,2048]{1,0:T(8,128)(2,1)} %constant_dynamic-update-slice_fusion, bf16[2048,384]{1,0:T(8,128)(2,1)} %bitcast.11), kind=kOutput, calls=%fused_computation.146 | convolution fusion | flops 3221225472 | bytes 13107200 | tf_op jit(solution)/shard_map/dot_general | solution.py:136
  182.2 5.0 fusion.3
  187.2 3.9 fusion.45
  191.3 19.0 %all_to_all.20 = bf16[8,128,128]{1,2,0:T(8,128)(2,1)S(1)} all-to-all(bf16[8,128,128]{1,2,0:T(8,128)(2,1)S(1)} %copy.45), channel_id=1, replica_groups={{0,4,8,12,16,20,24,28},{2,6,10,14,18,22,26,30},{1,5,9,13,17,21,25,29},{..., dimensions={0} | all-to-all | bytes 524288 | tf_op jit(solution)/shard_map/all_to_all | solution.py:144
  210.3 3.9 fusion.90
  214.8 18.0 %reduce-scatter.3.cloned.1.call-done = f32[128,1024]{1,0:T(8,128)} async-done(((f32[128,2048]{1,0:T(8,128)}), f32[128,1024]{1,0:T(8,128)}) %reduce-scatter.3.cloned.1.call-update) | async-done | bytes 524304 | tf_op jit(solution)/shard_map/reduce_scatter | solution.py:154
  234.7 7.3 %all-reduce = (f32[128]{0:T(128)S(1)}, f32[128,64]{0,1:T(8,128)S(1)}) all-reduce(f32[128]{0:T(128)S(1)} %get-tuple-element.7, f32[128,64]{0,1:T(8,128)S(1)} %fusion.50), channel_id=1, replica_groups=mesh['dp'=16,'mp'=2] {'mp'}, use_global_device_ids=true, to_apply=%region_12.13 | all-reduce | flops 8320 | bytes 66560 | tf_op jit(solution)/shard_map/psum | solution.py:159
  242.1 7.0 %all_gather.11 = bf16[128,2048]{1,0:T(8,128)(2,1)S(1)} all-gather(bf16[128,1024]{1,0:T(8,128)(2,1)S(1)} %fusion.51), channel_id=1, replica_groups=mesh['dp'=16,'mp'=2] {'mp'}, dimensions={1}, use_global_device_ids=true | all-gather | bytes 786432 | tf_op jit(solution)/shard_map/all_gather | solution.py:188
  250.4 98.4 %all_to_all.21 = bf16[16,2,32,2048]{3,2,1,0:T(8,128)(2,1)S(1)} all-to-all(bf16[16,2,32,2048]{3,2,1,0:T(8,128)(2,1)S(1)} %bitcast.92), channel_id=1, replica_groups=mesh['dp'=16,'mp'=2] {'dp'}, dimensions={0} | all-to-all | bytes 8388608 | tf_op jit(solution)/shard_map/all_to_all | solution.py:190
  352.5 3.8 fusion.11
  359.9 10.6 %fusion.21 = bf16[512,2048]{1,0:T(8,128)(2,1)} fusion(bf16[1,2048,2048]{2,1,0:T(8,128)(2,1)} %param.31, f32[512,1024]{1,0:T(8,128)} %fusion.11, bf16[512,2048]{1,0:T(8,128)(2,1)} %bitcast.99, bf16[2048,2048]{1,0:T(8,128)(2,1)} %bitcast.123), kind=kOutput, calls=%fused_computation.25 | convolution fusion | flops 4299161600 | bytes 14680064 | tf_op jit(solution)/shard_map/dot_general | solution.py:200
  370.5 10.6 %fusion.24 = bf16[512,2048]{1,0:T(8,128)(2,1)} fusion(bf16[1,2048,2048]{2,1,0:T(8,128)(2,1)} %param.31, f32[512,1024]{1,0:T(8,128)} %fusion.7, bf16[512,2048]{1,0:T(8,128)(2,1)} %bitcast.97, bf16[2048,2048]{1,0:T(8,128)(2,1)} %bitcast.124), kind=kOutput, calls=%fused_computation.26 | convolution fusion | flops 4299161600 | bytes 14680064 | tf_op jit(solution)/shard_map/dot_general | solution.py:200
  381.1 4.6 pad_maximum_fusion
  385.7 5.3 %all-to-all-start.3 = ((bf16[16,2,32,2048]{3,2,1,0:T(8,128)(2,1)}), bf16[16,2,32,2048]{3,2,1,0:T(8,128)(2,1)}, u32[]{:S(2)}, u32[]{:S(2)}) async-start(bf16[16,2,32,2048]{3,2,1,0:T(8,128)(2,1)} %pad_maximum_fusion), calls=%async_computation.4 | async-start | bytes 8388608 | tf_op jit(solution)/shard_map/all_to_all | solution.py:202
  391.1 77.5 %all-to-all-done.3 = bf16[16,2,32,2048]{3,2,1,0:T(8,128)(2,1)} async-done(((bf16[16,2,32,2048]{3,2,1,0:T(8,128)(2,1)}), bf16[16,2,32,2048]{3,2,1,0:T(8,128)(2,1)}, u32[]{:S(2)}, u32[]{:S(2)}) %all-to-all-start.3) | async-done | bytes 4194336 | tf_op jit(solution)/shard_map/all_to_all | solution.py:202
  471.7 3.9 fusion.27
  475.6 35.4 %reduce-scatter.5.cloned.1.call-done = f32[128,1024]{1,0:T(8,128)} async-done(((f32[128,2048]{1,0:T(8,128)}), f32[128,1024]{1,0:T(8,128)}) %reduce-scatter.5.cloned.1.call-update) | async-done | bytes 524304 | tf_op jit(solution)/shard_map/reduce_scatter | solution.py:213
  (138 shorter events, 70.4 us)
Async XLA Ops:
  6.5 227.5 %copy-start = (f32[1024,64]{0,1:T(8,128)S(1)}, f32[1024,64]{0,1:T(8,128)}, u32[]{:S(2)}) copy-start(f32[1024,64]{0,1:T(8,128)} %param.28) | copy-start | bytes 786436
  17.0 9.8 %copy-start.10 = (bf16[128,1024]{1,0:T(8,128)(2,1)S(1)}, bf16[128,1024]{1,0:T(8,128)(2,1)}, u32[]{:S(2)}) copy-start(bf16[128,1024]{1,0:T(8,128)(2,1)} %param.24) | copy-start | bytes 786436
  17.0 9.9 %copy-start.11 = (bf16[128,1024]{1,0:T(8,128)(2,1)S(1)}, bf16[128,1024]{1,0:T(8,128)(2,1)}, u32[]{:S(2)}) copy-start(bf16[128,1024]{1,0:T(8,128)(2,1)} %param.25) | copy-start | bytes 786436
  22.4 13.4 %collective-permute-start = (bf16[128,2048]{1,0:T(8,128)(2,1)S(1)}, bf16[128,2048]{1,0:T(8,128)(2,1)S(1)}, u32[]{:S(2)}, u32[]{:S(2)}) collective-permute-start(bf16[128,2048]{1,0:T(8,128)(2,1)S(1)} %get-tuple-element.10), channel_id=1, source_target_pairs={{0,2},{2,4},{4,6},{6,8},{8,10},{10,12},{12,14},{14,16},{16,18},{18... | collective-permute-start | bytes 1572872 | tf_op jit(solution)/shard_map/ppermute | solution.py:23
  22.4 13.7 %collective-permute-start.1 = (bf16[128,2048]{1,0:T(8,128)(2,1)S(1)}, bf16[128,2048]{1,0:T(8,128)(2,1)S(1)}, u32[]{:S(2)}, u32[]{:S(2)}) collective-permute-start(bf16[128,2048]{1,0:T(8,128)(2,1)S(1)} %get-tuple-element.10), channel_id=1, source_target_pairs={{0,30},{2,0},{4,2},{6,4},{8,6},{10,8},{12,10},{14,12},{16,14},{18,... | collective-permute-start | bytes 1572872 | tf_op jit(solution)/shard_map/ppermute | solution.py:26
  28.3 7.0 %copy-start.18 = (s32[4]{0:T(128)S(1)}, s32[4]{0:T(128)}, u32[]{:S(2)}) copy-start(s32[4]{0:T(128)} %param.17) | copy-start | bytes 52
  28.8 59.5 %copy-start.14 = (s32[2048]{0:T(1024)S(1)}, s32[2048]{0:T(1024)}, u32[]{:S(2)}) copy-start(s32[2048]{0:T(1024)} %param.18) | copy-start | bytes 24580
  30.1 132.7 %all-to-all-start = ((bf16[16,128,384]{2,1,0:T(8,128)(2,1)}), bf16[16,128,384]{2,1,0:T(8,128)(2,1)}, u32[]{:S(2)}, u32[]{:S(2)}) async-start(bf16[16,128,384]{2,1,0:T(8,128)(2,1)} %bitcast.10), calls=%async_computation | async-start | bytes 3145728 | tf_op jit(solution)/shard_map/all_to_all | solution.py:118
  34.6 175.7 %all-gather.2.cloned.1.call-start = ((), (), s32[]{:S(2)}) async-start(), calls=%async_computation.6 | async-start | bytes 4456448 | tf_op jit(solution)/shard_map/all_gather | solution.py:126
  35.3 197.5 %reduce-scatter.3.cloned.1.call-start = ((), (), s32[]{:S(2)}) async-start(), calls=%async_computation.7 | async-start | bytes 1572864 | tf_op jit(solution)/shard_map/reduce_scatter | solution.py:154
  35.8 44.3 %collective-permute-start.2 = (bf16[128,2048]{1,0:T(8,128)(2,1)S(1)}, bf16[128,2048]{1,0:T(8,128)(2,1)}, u32[]{:S(2)}, u32[]{:S(2)}) collective-permute-start(bf16[128,2048]{1,0:T(8,128)(2,1)S(1)} %collective-permute-done), channel_id=1, source_target_pairs={{0,2},{2,4},{4,6},{6,8},{8,10},{10,12},{12,14},{14,16},{16,18},{18... | collective-permute-start | bytes 1572872 | tf_op jit(solution)/shard_map/ppermute | solution.py:23
  36.1 47.7 %collective-permute-start.3 = (bf16[128,2048]{1,0:T(8,128)(2,1)S(1)}, bf16[128,2048]{1,0:T(8,128)(2,1)}, u32[]{:S(2)}, u32[]{:S(2)}) collective-permute-start(bf16[128,2048]{1,0:T(8,128)(2,1)S(1)} %collective-permute-done.1), channel_id=1, source_target_pairs={{0,30},{2,0},{4,2},{6,4},{8,6},{10,8},{12,10},{14,12},{16,14},{18,... | collective-permute-start | bytes 1572872 | tf_op jit(solution)/shard_map/ppermute | solution.py:26
  80.0 14.9 %collective-permute-start.4 = (bf16[128,2048]{1,0:T(8,128)(2,1)}, bf16[128,2048]{1,0:T(8,128)(2,1)}, u32[]{:S(2)}, u32[]{:S(2)}) collective-permute-start(bf16[128,2048]{1,0:T(8,128)(2,1)} %collective-permute-done.2), channel_id=1, source_target_pairs={{0,2},{2,4},{4,6},{6,8},{8,10},{10,12},{12,14},{14,16},{16,18},{18... | collective-permute-start | bytes 1572872 | tf_op jit(solution)/shard_map/ppermute | solution.py:23
  83.8 15.1 %collective-permute-start.5 = (bf16[128,2048]{1,0:T(8,128)(2,1)}, bf16[128,2048]{1,0:T(8,128)(2,1)}, u32[]{:S(2)}, u32[]{:S(2)}) collective-permute-start(bf16[128,2048]{1,0:T(8,128)(2,1)} %collective-permute-done.3), channel_id=1, source_target_pairs={{0,30},{2,0},{4,2},{6,4},{8,6},{10,8},{12,10},{14,12},{16,14},{18,... | collective-permute-start | bytes 1572872 | tf_op jit(solution)/shard_map/ppermute | solution.py:26
  95.0 15.2 %collective-permute-start.6 = (bf16[128,2048]{1,0:T(8,128)(2,1)}, bf16[128,2048]{1,0:T(8,128)(2,1)}, u32[]{:S(2)}, u32[]{:S(2)}) collective-permute-start(bf16[128,2048]{1,0:T(8,128)(2,1)} %collective-permute-done.4), channel_id=1, source_target_pairs={{0,2},{2,4},{4,6},{6,8},{8,10},{10,12},{12,14},{14,16},{16,18},{18... | collective-permute-start | bytes 1572872 | tf_op jit(solution)/shard_map/ppermute | solution.py:23
  98.8 15.2 %collective-permute-start.7 = (bf16[128,2048]{1,0:T(8,128)(2,1)}, bf16[128,2048]{1,0:T(8,128)(2,1)S(1)}, u32[]{:S(2)}, u32[]{:S(2)}) collective-permute-start(bf16[128,2048]{1,0:T(8,128)(2,1)} %collective-permute-done.5), channel_id=1, source_target_pairs={{0,30},{2,0},{4,2},{6,4},{8,6},{10,8},{12,10},{14,12},{16,14},{18,... | collective-permute-start | bytes 1572872 | tf_op jit(solution)/shard_map/ppermute | solution.py:26
  110.2 17.2 %collective-permute-start.8 = (bf16[128,2048]{1,0:T(8,128)(2,1)}, bf16[128,2048]{1,0:T(8,128)(2,1)S(1)}, u32[]{:S(2)}, u32[]{:S(2)}) collective-permute-start(bf16[128,2048]{1,0:T(8,128)(2,1)} %collective-permute-done.6), channel_id=1, source_target_pairs={{0,2},{2,4},{4,6},{6,8},{8,10},{10,12},{12,14},{14,16},{16,18},{18... | collective-permute-start | bytes 1572872 | tf_op jit(solution)/shard_map/ppermute | solution.py:23
  114.0 17.2 %collective-permute-start.9 = (bf16[128,2048]{1,0:T(8,128)(2,1)S(1)}, bf16[128,2048]{1,0:T(8,128)(2,1)S(1)}, u32[]{:S(2)}, u32[]{:S(2)}) collective-permute-start(bf16[128,2048]{1,0:T(8,128)(2,1)S(1)} %collective-permute-done.7), channel_id=1, source_target_pairs={{0,30},{2,0},{4,2},{6,4},{8,6},{10,8},{12,10},{14,12},{16,14},{18,... | collective-permute-start | bytes 1572872 | tf_op jit(solution)/shard_map/ppermute | solution.py:26
  127.5 11.4 %collective-permute-start.10 = (bf16[128,2048]{1,0:T(8,128)(2,1)S(1)}, bf16[128,2048]{1,0:T(8,128)(2,1)S(1)}, u32[]{:S(2)}, u32[]{:S(2)}) collective-permute-start(bf16[128,2048]{1,0:T(8,128)(2,1)S(1)} %collective-permute-done.8), channel_id=1, source_target_pairs={{0,2},{2,4},{4,6},{6,8},{8,10},{10,12},{12,14},{14,16},{16,18},{18... | collective-permute-start | bytes 1572872 | tf_op jit(solution)/shard_map/ppermute | solution.py:23
  131.3 11.1 %collective-permute-start.11 = (bf16[128,2048]{1,0:T(8,128)(2,1)S(1)}, bf16[128,2048]{1,0:T(8,128)(2,1)S(1)}, u32[]{:S(2)}, u32[]{:S(2)}) collective-permute-start(bf16[128,2048]{1,0:T(8,128)(2,1)S(1)} %collective-permute-done.9), channel_id=1, source_target_pairs={{0,30},{2,0},{4,2},{6,4},{8,6},{10,8},{12,10},{14,12},{16,14},{18,... | collective-permute-start | bytes 1572872 | tf_op jit(solution)/shard_map/ppermute | solution.py:26
  138.9 11.4 %collective-permute-start.12 = (bf16[128,2048]{1,0:T(8,128)(2,1)S(1)}, bf16[128,2048]{1,0:T(8,128)(2,1)S(1)}, u32[]{:S(2)}, u32[]{:S(2)}) collective-permute-start(bf16[128,2048]{1,0:T(8,128)(2,1)S(1)} %collective-permute-done.10), channel_id=1, source_target_pairs={{0,2},{2,4},{4,6},{6,8},{8,10},{10,12},{12,14},{14,16},{16,18},{18... | collective-permute-start | bytes 1572872 | tf_op jit(solution)/shard_map/ppermute | solution.py:23
  142.4 11.4 %collective-permute-start.13 = (bf16[128,2048]{1,0:T(8,128)(2,1)S(1)}, bf16[128,2048]{1,0:T(8,128)(2,1)S(1)}, u32[]{:S(2)}, u32[]{:S(2)}) collective-permute-start(bf16[128,2048]{1,0:T(8,128)(2,1)S(1)} %collective-permute-done.11), channel_id=1, source_target_pairs={{0,30},{2,0},{4,2},{6,4},{8,6},{10,8},{12,10},{14,12},{16,14},{18,... | collective-permute-start | bytes 1572872 | tf_op jit(solution)/shard_map/ppermute | solution.py:26
  150.3 11.7 %collective-permute-start.14 = (bf16[128,2048]{1,0:T(8,128)(2,1)S(1)}, bf16[128,2048]{1,0:T(8,128)(2,1)S(1)}, u32[]{:S(2)}, u32[]{:S(2)}) collective-permute-start(bf16[128,2048]{1,0:T(8,128)(2,1)S(1)} %collective-permute-done.12), channel_id=1, source_target_pairs={{0,2},{2,4},{4,6},{6,8},{8,10},{10,12},{12,14},{14,16},{16,18},{18... | collective-permute-start | bytes 1572872 | tf_op jit(solution)/shard_map/ppermute | solution.py:23
  162.9 8.0 %copy-start.17 = (f32[128]{0:T(128)S(1)}, f32[128]{0:T(128)}, u32[]{:S(2)}) copy-start(f32[128]{0:T(128)} %param.23) | copy-start | bytes 1540
  191.0 23.3 %copy-start.15 = (s32[128,8]{0,1:T(8,128)S(1)}, s32[128,8]{0,1:T(8,128)}, u32[]{:S(2)}) copy-start(s32[128,8]{0,1:T(8,128)} %param.19) | copy-start | bytes 12292
  191.0 41.8 %copy-start.7 = (bf16[128,1024]{1,0:T(8,128)(2,1)S(1)}, bf16[128,1024]{1,0:T(8,128)(2,1)}, u32[]{:S(2)}) copy-start(bf16[128,1024]{1,0:T(8,128)(2,1)} %param.16) | copy-start | bytes 786436
  191.2 42.8 %copy-start.12 = (f32[1024]{0:T(1024)S(1)}, f32[1024]{0:T(1024)}, u32[]{:S(2)}) copy-start(f32[1024]{0:T(1024)} %param.21) | copy-start | bytes 12292
  250.4 99.0 %slice-start = ((s8[8388608]{0:T(1024)(128)(4,1)}), s8[4194304]{0:T(1024)(128)(4,1)S(1)}, s32[]{:S(2)}) async-start(s8[8388608]{0:T(1024)(128)(4,1)} %bitcast.119), calls=%async_computation.9 | async-start | bytes 8388608
  349.4 6.9 %copy-start.6 = (bf16[16,1,32,2048]{3,2,1,0:T(8,128)(2,1)}, bf16[16,1,32,2048]{3,2,1,0:T(8,128)(2,1)S(1)}, u32[]{:S(2)}) copy-start(bf16[16,1,32,2048]{3,2,1,0:T(8,128)(2,1)S(1)} %get-tuple-element.11) | copy-start | bytes 6291460
  385.7 83.0 %all-to-all-start.3 = ((bf16[16,2,32,2048]{3,2,1,0:T(8,128)(2,1)}), bf16[16,2,32,2048]{3,2,1,0:T(8,128)(2,1)}, u32[]{:S(2)}, u32[]{:S(2)}) async-start(bf16[16,2,32,2048]{3,2,1,0:T(8,128)(2,1)} %pad_maximum_fusion), calls=%async_computation.4 | async-start | bytes 8388608 | tf_op jit(solution)/shard_map/all_to_all | solution.py:202
  391.0 120.1 %reduce-scatter.5.cloned.1.call-start = ((), (), s32[]{:S(2)}) async-start(), calls=%async_computation.8 | async-start | bytes 1572864 | tf_op jit(solution)/shard_map/reduce_scatter | solution.py:213
  468.7 44.2 %copy-start.1 = (f32[1024,64]{0,1:T(8,128)S(1)}, f32[1024,64]{0,1:T(8,128)}, u32[]{:S(2)}) copy-start(f32[1024,64]{0,1:T(8,128)} %param.28) | copy-start | bytes 786436
  (9 other events, 29.5 us)
Sparse Core Ops, SparseCore 0:
  37.6 86.9 all-gather.1
  214.3 18.4 reduce-scatter.2
  475.7 35.2 reduce-scatter.4
